TPU v7x, 32 devices: a whole 2x2x4 slice. The times are simulated.
32 devices in a mesh: kz: 4 (over x, core), tile: 8 (over z, y).
Axes of the slice: x: 2, y: 2, z: 4, core: 2. Of those that a mesh axis runs over, the one named last changes fastest.
Arguments:
- coil_data: bfloat16 [4, 8, 4, 8, 2, 16, 128], P('kz', 'tile'), may hold values from -6 to 6
- frame_of: int32 [4, 8, 4, 8, 2], P('kz', 'tile'), may hold values from 0 to 999
- basis: bfloat16 [1000, 10], replicated, may hold values from -4 to 4
- sample_pos: float32 [4, 8, 4, 8, 2, 2, 128], P('kz', 'tile'), may hold values from 1.5 to 30.5, as said below
- window_at: int32 [4, 8, 4, 8, 2, 2], P('kz', 'tile'), may hold values from -2 to 639, as said below
- live_count: int32 [4, 8, 4, 8], P('kz', 'tile'), may hold values from 0 to 2, as said below
Outputs:
- image: bfloat16 [4, 640, 102400], P('kz', None, 'tile')
Inputs may be any that keep to these rules, and one draw needn't show every extreme that they name: `live_count`: live slots of a pair are its first ones; destination tiles from 3 up to but not including 8 * 5 // 8 receive every slot from every acquiring device. `window_at`: the first entry (row0) lies in -2 to 78, the second (col0) in 0 to 639. `sample_pos`: the first entry lies in 1.5 to 2.5, the second in 1.5 to 32 - 1.5.
All inputs are finite; a program needn't handle non-finite values.
Results may differ from a plain program's by a relative error of at most 0.0077.
Values may be sent and summed in bfloat16 or wider, within the bound.
No kernel may reach another device: no remote copies, remote signals or barrier semaphores. Data moves between devices by JAX's collectives and lax.ppermute only.
A program may use at most 192 MiB of HBM per device.

v0:
```python
import math
import jax
import jax.numpy as jnp
from jax import lax
from jax.sharding import PartitionSpec as P

PLANE = 640
WIN_ROWS = 4
WIN_COLS = 32


def from_behind(value, axis, steps):
    count = lax.axis_size(axis)
    pairs = [(source, (source + steps) % count) for source in range(count)]
    return lax.ppermute(value, axis, pairs)


def taper(dist):
    inner = 1.0 - (dist / 1.5) ** 2
    return jnp.maximum(inner, 0.0) ** 2


def project(blocks, coeffs):
    count = blocks.shape[0]
    coils = blocks.shape[1] // 2
    ranks = coeffs.shape[1]
    samples = blocks.shape[2]
    data = blocks.astype(jnp.float32).reshape(count, 2, 1, coils, samples)
    scale = coeffs.astype(jnp.float32).reshape(count, 1, ranks, 1, 1)
    return (data * scale).reshape(count, 2 * ranks * coils, samples).astype(jnp.bfloat16)


def grid_tile(proj, offsets, corners, alive, tile_rows, plane):
    count, width, samples = proj.shape
    group = 64
    row_cells = jnp.arange(WIN_ROWS, dtype=jnp.float32)
    col_cells = jnp.arange(WIN_COLS, dtype=jnp.float32)
    cells = jnp.arange(WIN_ROWS * WIN_COLS, dtype=jnp.int32)
    cell_row = cells // WIN_COLS
    cell_col = cells % WIN_COLS

    def step(acc, items):
        values, place, corner, living = items
        row_k = taper(row_cells[None, :, None] - place[:, 0:1, :])
        col_k = taper(col_cells[None, :, None] - place[:, 1:2, :])
        weights = (row_k[:, :, None, :] * col_k[:, None, :, :]).reshape(
            group, WIN_ROWS * WIN_COLS, samples
        )
        weights = (weights * living[:, None, None]).astype(jnp.bfloat16)
        contrib = jnp.einsum("gwb,gcb->gwc", weights, values, preferred_element_type=jnp.float32)
        rows = corner[:, 0:1] + 2 + cell_row[None, :]
        cols = (corner[:, 1:2] + cell_col[None, :]) % plane
        acc = acc.at[rows.reshape(-1), cols.reshape(-1)].add(contrib.reshape(-1, width))
        return (acc, None)

    start = jnp.zeros((tile_rows + 4, plane, width), jnp.float32)
    items = (
        proj.reshape(-1, group, width, samples),
        offsets.reshape(-1, group, 2, samples),
        corners.reshape(-1, group, 2),
        alive.reshape(-1, group),
    )
    acc, _ = lax.scan(step, start, items)
    return acc


def tables(n):
    idx = jnp.arange(n, dtype=jnp.int32)
    phase = (idx[:, None] * idx[None, :] % n).astype(jnp.float32) * (2.0 * math.pi / n)
    return (jnp.cos(phase).astype(jnp.bfloat16), jnp.sin(phase).astype(jnp.bfloat16))


def combine(first, second, half):
    return jnp.concatenate(
        [first[..., :half] - second[..., half:], second[..., :half] + first[..., half:]], axis=-1
    )


def body(coil_data, frame_of, basis, sample_pos, window_at, live_count):
    parts = coil_data.shape[2]
    tiles = coil_data.shape[3]
    slots = coil_data.shape[4]
    pair = coil_data.shape[5]
    samples = coil_data.shape[6]
    width = 2 * basis.shape[1] * (pair // 2)
    half = width // 2
    tile_rows = PLANE // tiles
    raw = lax.all_to_all(
        lax.all_to_all(coil_data, "kz", split_axis=2, concat_axis=0, tiled=True),
        "tile",
        split_axis=3,
        concat_axis=1,
        tiled=True,
    )
    frames = lax.all_to_all(
        lax.all_to_all(frame_of, "kz", split_axis=2, concat_axis=0, tiled=True),
        "tile",
        split_axis=3,
        concat_axis=1,
        tiled=True,
    )
    arrived = project(raw.reshape(-1, pair, samples), basis[frames.reshape(-1)])
    slot_idx = jnp.arange(slots, dtype=jnp.int32)
    counts = live_count.reshape(parts, tiles)
    alive = (slot_idx[None, None, :] < counts[:, :, None]).astype(jnp.float32)
    acc = grid_tile(
        arrived,
        sample_pos.reshape(-1, 2, samples),
        window_at.reshape(-1, 2),
        alive.reshape(-1),
        tile_rows,
        PLANE,
    )
    from_above = from_behind(acc[tile_rows + 2 : tile_rows + 4], "tile", 1)
    from_below = from_behind(acc[0:2], "tile", -1)
    core = acc[2 : tile_rows + 2]
    core = core.at[0:2].add(from_above)
    core = core.at[tile_rows - 2 : tile_rows].add(from_below)
    grid = core.astype(jnp.bfloat16)
    cos_tab, sin_tab = tables(PLANE)
    first = jnp.einsum("xkq,ky->xyq", grid, cos_tab, preferred_element_type=jnp.float32)
    second = jnp.einsum("xkq,ky->xyq", grid, sin_tab, preferred_element_type=jnp.float32)
    mid = combine(first, second, half).astype(jnp.bfloat16)
    columns = lax.all_to_all(mid, "tile", split_axis=1, concat_axis=0, tiled=True)
    first = jnp.einsum("kyq,kx->xyq", columns, cos_tab, preferred_element_type=jnp.float32)
    second = jnp.einsum("kyq,kx->xyq", columns, sin_tab, preferred_element_type=jnp.float32)
    result = (combine(first, second, half) * (1.0 / PLANE)).astype(jnp.bfloat16)
    return result.reshape(1, result.shape[0], -1)


def solution(mesh):
    return jax.shard_map(
        body,
        mesh=mesh,
        in_specs=(
            P("kz", "tile", None, None, None, None, None),
            P("kz", "tile", None, None, None),
            P(),
            P("kz", "tile", None, None, None, None, None),
            P("kz", "tile", None, None, None, None),
            P("kz", "tile", None, None),
        ),
        out_specs=P("kz", None, "tile"),
        check_vma=False,
    )
```

profile of v0, /device:TPU:0, one launch (start us, length us, event | category | flops | bytes accessed | tf_op | source)
XLA Modules:
  0.0 1157.2 jit_solution(10622517823598696329)
XLA Ops:
  0.0 0.0 copy-start.2
  0.0 4.4 all-to-all-start.2
  4.4 0.8 copy.83
  5.2 0.1 squeeze.16
  5.3 0.1 add_remainder_fusion
  5.4 0.1 compare_select_fusion
  5.5 0.1 broadcast_add_fusion
  5.6 1.0 fusion.32
  6.6 0.2 maximum_multiply_fusion.1
  6.8 0.1 maximum_multiply_fusion.2
  6.9 2.6 broadcast_multiply_fusion
  9.5 0.8 fusion.17
  10.2 0.1 reshape.302
  10.3 0.0 all-to-all-done.2
  10.4 3.4 all-to-all-start
  13.8 2.6 fusion.6
  16.4 0.0 copy-done.2
  16.4 0.2 and_reduce_fusion
  16.6 0.7 copy.89
  17.3 2.5 all-to-all-done
  19.8 6.3 all-to-all-start.3
  26.1 0.0 copy-done.1
  26.1 0.1 multiply_reduce_fusion
  26.3 0.0 copy-done
  26.3 0.2 copy.91
  26.5 0.7 copy.85
  27.2 5.4 all-to-all-done.3
  32.6 3.4 all-to-all-start.1
  36.0 0.1 copy.90
  36.2 0.1 reshape.292
  36.3 0.6 gather_fusion
  37.0 0.1 copy.92
  37.1 0.1 copy.93
  37.2 7.0 all-to-all-done.1
  44.3 1.7 fusion.5
  45.9 5.1 fusion.33
  51.0 66.4 %scatter_custom_fusion = f32[53760,160]{1,0:T(8,128)} fusion(s32[8192]{0:T(1024)S(1)} %broadcast_select_fusion, f32[8192,160]{1,0:T(8,128)} %bitcast.76, f32[]{:T(128)} %constant.134.clone.1), kind=kCustom, calls=%fused_computation.4 | custom fusion | flops 1310720 | bytes 34406912
  117.4 3.5 fusion.31
  121.0 2.4 copy.110
  123.4 0.2 collective-permute-start
  123.5 1.3 copy.111
  124.9 4.6 collective-permute-start.1
  129.4 34.4 %slice.123 = f32[51200,160]{1,0:T(8,128)} slice(f32[53760,160]{1,0:T(8,128)} %scatter_custom_fusion), slice={[1280:52480], [0:160]} | slice | bytes 65536000 | tf_op jit(solution)/shard_map/slice | solution.py:116
  163.8 0.8 copy.109
  164.7 52.2 %copy.108 = f32[80,640,160]{1,0,2:T(8,128)} copy(f32[80,640,160]{2,1,0:T(8,128)} %bitcast.66) | data formatting | bytes 65536000 | tf_op jit(solution)/shard_map/slice | solution.py:116
  216.9 0.0 collective-permute-done
  216.9 2.5 add_dynamic-update-slice_fusion
  219.4 0.0 collective-permute-done.1
  219.4 3.4 fusion.12
  222.8 11.5 convert_element_type.79
  234.3 9.7 copy.100
  244.0 30.4 %fusion.13 = f32[640,12800]{0,1} fusion(bf16[640,12800]{0,1:T(8,128)(2,1)} %bitcast.74), kind=kOutput, calls=%fused_computation.31 | convolution fusion | flops 10489856000 | bytes 49152000
  274.5 30.5 %fusion.15 = f32[640,12800]{0,1} fusion(bf16[640,12800]{0,1:T(8,128)(2,1)} %bitcast.75), kind=kOutput, calls=%fused_computation.33 | convolution fusion | flops 10489856000 | bytes 49152000
  305.0 24.4 %fusion.4 = (bf16[80,640,80]{1,2,0:T(8,128)(2,1)S(1)}, bf16[80,640,80]{1,2,0:T(8,128)(2,1)}) fusion(f32[80,640,160]{1,2,0:T(8,128)} %bitcast.71, f32[80,640,160]{1,2,0:T(8,128)} %bitcast.70), kind=kLoop, calls=%fused_computation.11 | loop fusion | flops 16384000 | bytes 81920000 | tf_op jit(solution)/shard_map/convert.2
  329.4 10.3 pad_maximum_fusion
  339.7 38.3 %copy.102 = bf16[80,640,160]{2,0,1:T(8,128)(2,1)} copy(bf16[80,640,160]{1,2,0:T(8,128)(2,1)} %pad_maximum_fusion) | data formatting | bytes 32768000 | tf_op jit(solution)/shard_map/concatenate | solution.py:74
  378.0 571.9 %all_to_all.60 = bf16[80,640,160]{2,0,1:T(8,128)(2,1)} all-to-all(bf16[80,640,160]{2,0,1:T(8,128)(2,1)} %copy.102), channel_id=1, replica_groups=mesh['kz'=4,'tile'=8] {'tile'}, dimensions={1} | all-to-all | bytes 32768000 | tf_op jit(solution)/shard_map/all_to_all | solution.py:124
  950.0 36.0 %copy.103 = bf16[80,8,80,160]{0,1,3,2:T(8,128)(2,1)} copy(bf16[80,8,80,160]{3,0,2,1:T(8,128)(2,1)} %bitcast.67) | data formatting | bytes 32768000 | tf_op jit(solution)/shard_map/all_to_all | solution.py:124
  986.0 37.6 %reshape.322 = bf16[640,12800]{0,1:T(8,128)(2,1)} reshape(bf16[8,80,80,160]{1,0,3,2:T(8,128)(2,1)} %bitcast.68) | data formatting | bytes 32768000
  1023.5 30.4 %fusion.14 = f32[640,12800]{0,1} fusion(bf16[640,12800]{0,1:T(8,128)(2,1)} %reshape.322), kind=kOutput, calls=%fused_computation.32 | convolution fusion | flops 10489856000 | bytes 49152000
  1054.0 30.5 %fusion.16 = f32[640,12800]{0,1} fusion(bf16[640,12800]{0,1:T(8,128)(2,1)} %reshape.322), kind=kOutput, calls=%fused_computation.34 | convolution fusion | flops 10489856000 | bytes 49152000
  1084.5 33.0 %slice_subtract_fusion = (f32[640,80,80]{0,2,1:T(8,128)}, f32[640,80,80]{0,2,1:T(8,128)}) fusion(f32[640,80,160]{0,2,1:T(8,128)} %bitcast.73, f32[640,80,160]{0,2,1:T(8,128)} %bitcast.72), kind=kLoop, calls=%fused_computation.7 | loop fusion | flops 8192000 | bytes 98304000 | tf_op jit(solution)/shard_map/sub | solution.py:75
  1117.5 17.7 %fusion = bf16[640,80,160]{0,2,1:T(8,128)(2,1)} fusion(f32[640,80,80]{0,2,1:T(8,128)} %get-tuple-element.60, f32[640,80,80]{0,2,1:T(8,128)} %get-tuple-element.59), kind=kLoop, calls=%fused_computation.3 | loop fusion | flops 24576000 | bytes 49152000 | tf_op jit(solution)/shard_map/convert_element_type | solution.py:127
  1135.2 21.9 %copy.104 = bf16[1,640,12800]{2,1,0:T(8,128)(2,1)} copy(bf16[1,640,12800]{1,2,0:T(8,128)(2,1)} %bitcast.69) | data formatting | bytes 32768000 | tf_op jit(solution)/shard_map/convert_element_type | solution.py:127
  (11 shorter events, 0.1 us)
Async XLA Ops:
  0.0 16.4 %copy-start.2 = (s32[2]{0:T(128)S(1)}, s32[2]{0:T(128)}, u32[]{:S(2)}) copy-start(s32[2]{0:T(128)} %constant.155) | copy-start | bytes 28
  0.0 26.1 %copy-start.1 = (s32[2]{0:T(128)S(1)}, s32[2]{0:T(128)}, u32[]{:S(2)}) copy-start(s32[2]{0:T(128)} %constant.152) | copy-start | bytes 28
  0.0 26.2 %copy-start = (bf16[1000,10]{0,1:T(8,128)(2,1)S(1)}, bf16[1000,10]{0,1:T(8,128)(2,1)}, u32[]{:S(2)}) copy-start(bf16[1000,10]{0,1:T(8,128)(2,1)} %param.12) | copy-start | bytes 60004
  0.0 10.3 all-to-all-start.2
  10.4 9.4 all-to-all-start
  19.8 12.9 %all-to-all-start.3 = ((s32[4,1,1,8,2]{0,4,2,1,3:T(2,128)}), s32[4,1,1,8,2]{0,4,2,1,3:T(2,128)S(1)}, u32[]{:S(2)}, u32[]{:S(2)}) async-start(s32[4,1,1,8,2]{0,4,2,1,3:T(2,128)} %copy.89), calls=%async_computation.3 | async-start | bytes 16384 | tf_op jit(solution)/shard_map/all_to_all | solution.py:95
  32.6 11.6 %all-to-all-start.1 = ((bf16[4,1,1,8,2,16,128]{6,5,4,0,2,1,3:T(8,128)(2,1)}), bf16[4,1,1,8,2,16,128]{6,5,4,0,2,1,3:T(8,128)(2,1)S(1)}, u32[]{:S(2)}, u32[]{:S(2)}) async-start(bf16[4,1,1,8,2,16,128]{6,5,4,0,2,1,3:T(8,128)(2,1)} %copy.85), calls=%async_computation.1 | async-start | bytes 524288 | tf_op jit(solution)/shard_map/all_to_all | solution.py:88
  123.4 93.5 %collective-permute-start = (f32[2,640,160]{1,0,2:T(2,128)}, f32[2,640,160]{1,0,2:T(2,128)}, u32[]{:S(2)}, u32[]{:S(2)}) collective-permute-start(f32[2,640,160]{1,0,2:T(2,128)} %copy.110), channel_id=1, source_target_pairs={{0,1},{1,2},{2,3},{3,4},{4,5},{5,6},{6,7},{7,0},{8,9},{9,10},{10,1... | collective-permute-start | bytes 2457608 | tf_op jit(solution)/shard_map/ppermute | solution.py:15
  124.9 94.6 %collective-permute-start.1 = (f32[2,640,160]{1,0,2:T(2,128)}, f32[2,640,160]{1,0,2:T(2,128)S(1)}, u32[]{:S(2)}, u32[]{:S(2)}) collective-permute-start(f32[2,640,160]{1,0,2:T(2,128)} %copy.111), channel_id=1, source_target_pairs={{0,7},{1,0},{2,1},{3,2},{4,3},{5,4},{6,5},{7,6},{8,15},{9,8},{10,9... | collective-permute-start | bytes 2457608 | tf_op jit(solution)/shard_map/ppermute | solution.py:15
where the time goes:
time: 1170 us; the launch traced here: 1160 us
  blocking collectives  572 us (49%)
  local copies, waits for them, and re-layouts  243 us (21%)
  other arithmetic  178 us (15%)
  matrix products  127 us (11%)
  starting transfers between devices  22.3 us (2%)
  waiting for transfers between devices  15 us (1%)
    all_to_all x1, blocking collectives, body(): lax.all_to_all(mid, 'tile', split_axis=1, concat_axis=0, tiled=True)  572 us
    unnamed x4, matrix products  122 us
    slice x2, local copies, waits for them, and re-layouts, body(): core = acc[2:tile_rows + 2]  86.6 us
    unnamed x4, other arithmetic  66.7 us
    unnamed x9, local copies, waits for them, and re-layouts  38.6 us
    concatenate x1, local copies, waits for them, and re-layouts, combine(): jnp.concatenate([first[..., :half] - second[..., half:], second[..., :hal...  38.3 us
    all_to_all x1, local copies, waits for them, and re-layouts, body(): lax.all_to_all(mid, 'tile', split_axis=1, concat_axis=0, tiled=True)  36 us
    sub x1, other arithmetic, combine(): first[..., :half] - second[..., half:]  33 us
  transfers between devices with their start and end apart: 6, of which 3 were waited for; matrix products, arithmetic and copies ran while one was open for 9% of the time, Pallas kernels for 0%

commit v1 on v0

--- a/solution.py
+++ b/solution.py
@@ -121,7 +121,10 @@
     first = jnp.einsum("xkq,ky->xyq", grid, cos_tab, preferred_element_type=jnp.float32)
     second = jnp.einsum("xkq,ky->xyq", grid, sin_tab, preferred_element_type=jnp.float32)
     mid = combine(first, second, half).astype(jnp.bfloat16)
-    columns = lax.all_to_all(mid, "tile", split_axis=1, concat_axis=0, tiled=True)
+    size = lax.axis_size("tile")
+    pieces = jnp.stack(jnp.split(mid, size, axis=1), axis=0)
+    pieces = lax.all_to_all(pieces, "tile", split_axis=0, concat_axis=0)
+    columns = jnp.concatenate(pieces, axis=0)
     first = jnp.einsum("kyq,kx->xyq", columns, cos_tab, preferred_element_type=jnp.float32)
     second = jnp.einsum("kyq,kx->xyq", columns, sin_tab, preferred_element_type=jnp.float32)
     result = (combine(first, second, half) * (1.0 / PLANE)).astype(jnp.bfloat16)

time: 1170 us -> 1110 us (0.949)
  local copies, waits for them, and re-layouts: 243 us -> 168 us
  other arithmetic: 178 us -> 190 us
    concatenate x1 -> x0, local copies, waits for them, and re-layouts: 38.3 us -> none  [combine(): jnp.concatenate([first[..., :half] - second[..., half:], second[..., :hal...]
    all_to_all x1 -> x0, local copies, waits for them, and re-layouts: 36 us -> none  [body(): lax.all_to_all(mid, 'tile', split_axis=1, concat_axis=0, tiled=True)]
    unnamed x9 -> x10, local copies, waits for them, and re-layouts: 38.6 us -> 2.86 us
    reshape x0 -> x1, local copies, waits for them, and re-layouts: none -> 35.2 us  [body(): columns = jnp.concatenate(pieces, axis=0)]
    unnamed x4 -> x11, other arithmetic: 66.7 us -> 86.4 us
    another operation x1 -> x2, other arithmetic: 24.4 us -> 27.1 us
where the time goes in v1:
time: 1110 us; the launch traced here: 1100 us
  blocking collectives  572 us (52%)
  other arithmetic  190 us (17%)
  local copies, waits for them, and re-layouts  168 us (15%)
  matrix products  135 us (12%)
  starting transfers between devices  22.3 us (2%)
  waiting for transfers between devices  15 us (1%)
    all_to_all x1, blocking collectives, body(): pieces = lax.all_to_all(pieces, 'tile', split_axis=0, concat_axis=0)  572 us
    unnamed x4, matrix products  130 us
    slice x2, local copies, waits for them, and re-layouts, body(): core = acc[2:tile_rows + 2]  86.6 us
    unnamed x11, other arithmetic  86.4 us
    reshape x1, local copies, waits for them, and re-layouts, body(): columns = jnp.concatenate(pieces, axis=0)  35.2 us
    sub x1, other arithmetic, combine(): first[..., :half] - second[..., half:]  33 us
    another operation x1, other arithmetic  24.4 us
  transfers between devices with their start and end apart: 6, of which 3 were waited for; matrix products, arithmetic and copies ran while one was open for 9% of the time, Pallas kernels for 0%

profile of v1, /device:TPU:0, one launch (start us, length us, event | category | flops | bytes accessed | tf_op | source)
XLA Modules:
  0.0 1102.2 jit_solution(10829402923318572074)
XLA Ops:
  0.0 4.4 all-to-all-start.2
  4.4 0.8 copy.86
  5.2 0.1 squeeze.16
  5.3 0.1 add_remainder_fusion
  5.4 0.1 compare_select_fusion
  5.5 0.1 broadcast_add_fusion
  5.6 1.0 fusion.55
  6.6 0.2 maximum_multiply_fusion.1
  6.8 0.1 maximum_multiply_fusion.2
  6.9 2.6 broadcast_multiply_fusion
  9.5 0.8 fusion.40
  10.2 0.1 reshape.306
  10.3 0.0 all-to-all-done.2
  10.4 3.4 all-to-all-start
  13.8 2.6 fusion.6
  16.4 0.2 and_reduce_fusion
  16.6 0.7 copy.92
  17.3 2.5 all-to-all-done
  19.8 6.3 all-to-all-start.3
  26.1 0.1 multiply_reduce_fusion
  26.3 0.2 copy.94
  26.5 0.7 copy.88
  27.2 5.4 all-to-all-done.3
  32.6 3.4 all-to-all-start.1
  36.0 0.1 copy.93
  36.2 0.1 reshape.295
  36.3 0.6 gather_fusion
  37.0 0.1 copy.95
  37.1 0.1 copy.96
  37.2 7.0 all-to-all-done.1
  44.3 1.7 fusion.5
  45.9 5.1 fusion.56
  51.1 66.5 %scatter_custom_fusion = f32[53760,160]{1,0:T(8,128)} fusion(s32[8192]{0:T(1024)S(1)} %broadcast_select_fusion, f32[8192,160]{1,0:T(8,128)} %bitcast.106, f32[]{:T(128)} %constant.134.clone.1), kind=kCustom, calls=%fused_computation.18 | custom fusion | flops 1310720 | bytes 34406912
  117.5 3.5 fusion.54
  121.0 2.4 copy.113
  123.4 0.1 collective-permute-start
  123.6 1.3 copy.114
  124.9 4.6 collective-permute-start.1
  129.5 34.4 %slice.123 = f32[51200,160]{1,0:T(8,128)} slice(f32[53760,160]{1,0:T(8,128)} %scatter_custom_fusion), slice={[1280:52480], [0:160]} | slice | bytes 65536000 | tf_op jit(solution)/shard_map/slice | solution.py:116
  163.9 0.8 copy.112
  164.7 52.2 %copy.111 = f32[80,640,160]{1,0,2:T(8,128)} copy(f32[80,640,160]{2,1,0:T(8,128)} %bitcast.95) | data formatting | bytes 65536000 | tf_op jit(solution)/shard_map/slice | solution.py:116
  217.0 2.6 add_dynamic-update-slice_fusion
  219.6 3.4 fusion.35
  222.9 11.5 %convert_element_type.79 = bf16[80,640,160]{1,0,2:T(8,128)(2,1)S(1)} convert(f32[80,640,160]{1,0,2:T(8,128)} %fusion.35) | non-fusion elementwise | flops 8192000 | bytes 49152000 | tf_op jit(solution)/shard_map/convert_element_type | solution.py:119
  234.5 9.7 copy.103
  244.2 30.3 %fusion.36 = f32[640,12800]{0,1} fusion(bf16[640,12800]{0,1:T(8,128)(2,1)} %bitcast.102), kind=kOutput, calls=%fused_computation.68 | convolution fusion | flops 10489856000 | bytes 49152000
  274.5 38.4 %fusion.38 = f32[640,12800]{0,1} fusion(bf16[640,12800]{0,1:T(8,128)(2,1)} %bitcast.103), kind=kOutput, calls=%fused_computation.70 | convolution fusion | flops 10489856000 | bytes 49152000
  312.9 24.4 %fusion.3 = (bf16[80,640,80]{1,2,0:T(8,128)(2,1)S(1)}, bf16[80,640,80]{1,2,0:T(8,128)(2,1)}) fusion(f32[80,640,160]{1,2,0:T(8,128)} %bitcast.98, f32[80,640,160]{1,2,0:T(8,128)} %bitcast.99), kind=kLoop, calls=%fused_computation.23 | loop fusion | flops 16384000 | bytes 81920000 | tf_op jit(solution)/shard_map/convert.3
  337.3 3.2 fusion.12
  340.5 1.8 copy-done
  342.3 2.7 fusion.15
  345.0 2.7 fusion.18
  347.8 2.8 fusion.21
  350.5 2.9 fusion.24
  353.4 2.6 fusion.27
  356.1 2.7 fusion.9
  358.8 2.7 fusion.29
  361.4 571.5 %all_to_all.47 = bf16[8,80,80,160]{2,3,1,0:T(8,128)(2,1)} all-to-all(bf16[8,80,80,160]{2,3,1,0:T(8,128)(2,1)} %fusion.29), channel_id=1, replica_groups=mesh['kz'=4,'tile'=8] {'tile'}, dimensions={0} | all-to-all | bytes 32768000 | tf_op jit(solution)/shard_map/all_to_all | solution.py:126
  933.0 35.2 %copy.105 = bf16[640,80,160]{0,2,1:T(8,128)(2,1)} copy(bf16[640,80,160]{1,2,0:T(8,128)(2,1)} %bitcast.96) | data formatting | bytes 32768000 | tf_op jit(solution)/shard_map/reshape | solution.py:127
  968.2 30.3 %fusion.37 = f32[640,12800]{0,1} fusion(bf16[640,12800]{0,1:T(8,128)(2,1)} %bitcast.104), kind=kOutput, calls=%fused_computation.69 | convolution fusion | flops 10489856000 | bytes 49152000
  998.5 30.6 %fusion.39 = f32[640,12800]{0,1} fusion(bf16[640,12800]{0,1:T(8,128)(2,1)} %bitcast.105), kind=kOutput, calls=%fused_computation.71 | convolution fusion | flops 10489856000 | bytes 49152000
  1029.1 33.0 %slice_subtract_fusion = (f32[640,80,80]{0,2,1:T(8,128)}, f32[640,80,80]{0,2,1:T(8,128)}) fusion(f32[640,80,160]{0,2,1:T(8,128)} %bitcast.101, f32[640,80,160]{0,2,1:T(8,128)} %bitcast.100), kind=kLoop, calls=%fused_computation.21 | loop fusion | flops 8192000 | bytes 98304000 | tf_op jit(solution)/shard_map/sub | solution.py:75
  1062.2 17.7 %fusion = bf16[640,80,160]{0,2,1:T(8,128)(2,1)} fusion(f32[640,80,80]{0,2,1:T(8,128)} %get-tuple-element.60, f32[640,80,80]{0,2,1:T(8,128)} %get-tuple-element.59), kind=kLoop, calls=%fused_computation.3 | loop fusion | flops 24576000 | bytes 49152000 | tf_op jit(solution)/shard_map/convert_element_type | solution.py:130
  1079.9 21.9 %copy.107 = bf16[1,640,12800]{2,1,0:T(8,128)(2,1)} copy(bf16[1,640,12800]{1,2,0:T(8,128)(2,1)} %bitcast.97) | data formatting | bytes 32768000 | tf_op jit(solution)/shard_map/convert_element_type | solution.py:130
  (18 shorter events, 0.2 us)
Async XLA Ops:
  0.0 16.4 %copy-start.3 = (s32[2]{0:T(128)S(1)}, s32[2]{0:T(128)}, u32[]{:S(2)}) copy-start(s32[2]{0:T(128)} %constant.155) | copy-start | bytes 28
  0.0 26.1 %copy-start.2 = (s32[2]{0:T(128)S(1)}, s32[2]{0:T(128)}, u32[]{:S(2)}) copy-start(s32[2]{0:T(128)} %constant.152) | copy-start | bytes 28
  0.0 26.2 %copy-start.1 = (bf16[1000,10]{0,1:T(8,128)(2,1)S(1)}, bf16[1000,10]{0,1:T(8,128)(2,1)}, u32[]{:S(2)}) copy-start(bf16[1000,10]{0,1:T(8,128)(2,1)} %param.12) | copy-start | bytes 60004
  0.0 10.3 all-to-all-start.2
  10.4 9.4 all-to-all-start
  19.8 12.9 %all-to-all-start.3 = ((s32[4,1,1,8,2]{0,4,2,1,3:T(2,128)}), s32[4,1,1,8,2]{0,4,2,1,3:T(2,128)S(1)}, u32[]{:S(2)}, u32[]{:S(2)}) async-start(s32[4,1,1,8,2]{0,4,2,1,3:T(2,128)} %copy.92), calls=%async_computation.3 | async-start | bytes 16384 | tf_op jit(solution)/shard_map/all_to_all | solution.py:95
  32.6 11.6 %all-to-all-start.1 = ((bf16[4,1,1,8,2,16,128]{6,5,4,0,2,1,3:T(8,128)(2,1)}), bf16[4,1,1,8,2,16,128]{6,5,4,0,2,1,3:T(8,128)(2,1)S(1)}, u32[]{:S(2)}, u32[]{:S(2)}) async-start(bf16[4,1,1,8,2,16,128]{6,5,4,0,2,1,3:T(8,128)(2,1)} %copy.88), calls=%async_computation.1 | async-start | bytes 524288 | tf_op jit(solution)/shard_map/all_to_all | solution.py:88
  123.4 93.5 %collective-permute-start = (f32[2,640,160]{1,0,2:T(2,128)}, f32[2,640,160]{1,0,2:T(2,128)}, u32[]{:S(2)}, u32[]{:S(2)}) collective-permute-start(f32[2,640,160]{1,0,2:T(2,128)} %copy.113), channel_id=1, source_target_pairs={{0,1},{1,2},{2,3},{3,4},{4,5},{5,6},{6,7},{7,0},{8,9},{9,10},{10,1... | collective-permute-start | bytes 2457608 | tf_op jit(solution)/shard_map/ppermute | solution.py:15
  124.9 94.6 %collective-permute-start.1 = (f32[2,640,160]{1,0,2:T(2,128)}, f32[2,640,160]{1,0,2:T(2,128)S(1)}, u32[]{:S(2)}, u32[]{:S(2)}) collective-permute-start(f32[2,640,160]{1,0,2:T(2,128)} %copy.114), channel_id=1, source_target_pairs={{0,7},{1,0},{2,1},{3,2},{4,3},{5,4},{6,5},{7,6},{8,15},{9,8},{10,9... | collective-permute-start | bytes 2457608 | tf_op jit(solution)/shard_map/ppermute | solution.py:15
  337.3 5.0 copy-start
